TPU v7x, 512 devices: a whole 4x8x8 slice. The times are simulated.
512 devices in a mesh: tok: 16 (over z, core), voc: 32 (over y, x).
Axes of the slice: x: 4, y: 8, z: 8, core: 2. Of those that a mesh axis runs over, the one named last changes fastest.
Arguments:
- hidden: bfloat16 [256, 2304], P('tok', 'voc'), may hold values from -18 to 18
- head: bfloat16 [2304, 131072], P(None, ('tok', 'voc')), as said below
- targets: int32 [256], replicated, may hold values from 0 to 131071
- probe_hidden: bfloat16 [256, 2304], P('tok', 'voc'), may hold values from -6 to 6
- probe_head: bfloat16 [2304, 131072], P(None, ('tok', 'voc')), may hold values from -0.5 to 0.5
Outputs:
- head_out: float32 [2304, 131072], P(None, ('tok', 'voc'))
- hidden_out: float32 [256, 2304], P('tok', 'voc')
Inputs may be any that keep to these rules, and one draw needn't show every extreme that they name: `head`: entries lie within 66 / sqrt(2304) in magnitude.
All inputs are finite; a program needn't handle non-finite values.
Results may differ from a plain program's by a relative error of at most 0.0075.
Values may be sent and summed in bfloat16 or wider, within the bound.
A program may use at most 64 MiB of HBM per device.

v0:
```python
import jax
import jax.numpy as jnp
from jax import lax
import numpy as np
from jax.sharding import Mesh, PartitionSpec as P

softcap_value = 30.0
zloss_weight = 0.0001


def local(hidden, head, targets, probe_hidden, probe_head):
    voc_count = lax.axis_size("vy") * lax.axis_size("vx")
    vocab_width = head.shape[1]
    rows_here = hidden.shape[0]
    stacked = jnp.stack([hidden, probe_hidden])
    copies = jnp.broadcast_to(stacked[None], (voc_count,) + stacked.shape)
    blocks = lax.all_to_all(copies, ("vy", "vx"), 0, 0, tiled=True)
    features = blocks.transpose(1, 2, 0, 3).reshape(2, rows_here, voc_count * stacked.shape[2])
    gathered = lax.all_gather(features, "tok", axis=1, tiled=True)
    row_hidden = gathered[0]
    row_probe = gathered[1]
    logits = jnp.dot(row_hidden, head, preferred_element_type=jnp.float32)
    tangent = jnp.dot(row_probe, head, preferred_element_type=jnp.float32) + jnp.dot(
        row_hidden, probe_head, preferred_element_type=jnp.float32
    )
    capped = jnp.tanh(logits / softcap_value)
    cap_slope = 1.0 - capped * capped
    exponent = jnp.exp(softcap_value * capped)
    cap_tangent = cap_slope * tangent
    slope_tan = -2.0 / softcap_value * capped * cap_slope * tangent
    voc_index = lax.axis_index("vy") * lax.axis_size("vx") + lax.axis_index("vx")
    offset = (lax.axis_index("tok") * voc_count + voc_index) * vocab_width
    columns = offset + lax.iota(jnp.int32, vocab_width)
    onehot = (targets[:, None] == columns[None, :]).astype(jnp.float32)
    weighted_slope = exponent * cap_slope
    weighted_tan = exponent * (cap_slope * cap_tangent + slope_tan)
    hi = lax.Precision.HIGH
    by_probe = lax.dot_general(
        jnp.stack([weighted_slope, onehot * cap_slope]),
        probe_head.astype(jnp.float32),
        (((2,), (1,)), ((), ())),
        precision=hi,
        preferred_element_type=jnp.float32,
    )
    by_head = lax.dot_general(
        jnp.stack([weighted_tan, weighted_slope, onehot * slope_tan]),
        head.astype(jnp.float32),
        (((2,), (1,)), ((), ())),
        precision=hi,
        preferred_element_type=jnp.float32,
    )
    partials = jnp.stack([by_probe[0] + by_head[0], by_head[1], by_probe[1] + by_head[2]])
    local_stats = jnp.stack([jnp.sum(exponent, axis=1), jnp.sum(exponent * cap_tangent, axis=1)])
    partials, local_stats = lax.optimization_barrier((partials, local_stats))
    summed = lax.psum_scatter(partials, "tok", scatter_dimension=1, tiled=True)
    stats = lax.psum(lax.psum(lax.psum(local_stats, "tok"), "vy"), "vx")
    kinds, rows, width = summed.shape
    blocks = summed.reshape(kinds, rows, voc_count, width // voc_count).transpose(2, 0, 1, 3)
    reduced = jnp.sum(lax.all_to_all(blocks, ("vy", "vx"), 0, 0, tiled=True), axis=0)
    row_total = stats[0]
    probability = exponent / row_total[:, None]
    mean_tangent = stats[1] / row_total
    factor = 1.0 + 2.0 * zloss_weight * jnp.log(row_total)
    grad_cap = factor[:, None] * probability - onehot
    grad_tan = probability * (
        factor[:, None] * (cap_tangent - mean_tangent[:, None])
        + 2.0 * zloss_weight * mean_tangent[:, None]
    )
    dlogit = (grad_cap * cap_slope).astype(jnp.bfloat16)
    dlogit_tan = (grad_tan * cap_slope + grad_cap * slope_tan).astype(jnp.bfloat16)
    head_out = jnp.einsum(
        "krd,krv->dv", gathered, jnp.stack([dlogit_tan, dlogit]), preferred_element_type=jnp.float32
    )
    first_row = lax.axis_index("tok") * rows_here
    own_total = lax.dynamic_slice_in_dim(row_total, first_row, rows_here)
    own_mean = lax.dynamic_slice_in_dim(mean_tangent, first_row, rows_here)
    own_factor = lax.dynamic_slice_in_dim(factor, first_row, rows_here)
    scale_main = (own_factor / own_total)[:, None]
    scale_mean = ((2.0 * zloss_weight - own_factor) * own_mean / own_total)[:, None]
    hidden_out = scale_main * reduced[0] + scale_mean * reduced[1] - reduced[2]
    return (head_out, hidden_out)


def solution(mesh):
    tok_size, voc_size = mesh.devices.shape
    x_size = 4 if voc_size % 4 == 0 else 1
    split = Mesh(
        np.asarray(mesh.devices).reshape(tok_size, voc_size // x_size, x_size), ("tok", "vy", "vx")
    )
    voc = ("vy", "vx")
    return jax.shard_map(
        local,
        mesh=split,
        in_specs=(
            P("tok", voc),
            P(None, ("tok",) + voc),
            P(),
            P("tok", voc),
            P(None, ("tok",) + voc),
        ),
        out_specs=(P(None, ("tok",) + voc), P("tok", voc)),
        check_vma=False,
    )
```

profile of v0, /device:TPU:2, one launch (start us, length us, event | category | flops | bytes accessed | tf_op | source)
XLA Modules:
  0.0 204.7 jit_solution(5712569975829166852)
XLA Ops:
  7.2 0.0 copy-start
  7.2 0.0 all-gather.2.cloned.1.call-start
  7.2 0.8 pad_maximum_fusion.1
  8.1 21.4 %all_to_all.10 = bf16[32,2,16,72]{3,2,1,0:T(8,128)(2,1)S(1)} all-to-all(bf16[32,2,16,72]{3,2,1,0:T(8,128)(2,1)S(1)} %broadcast_in_dim.2), channel_id=1, replica_groups=mesh['tok'=16,'vy'=8,'vx'=4] {'vy','vx'}, dimensions={0} | all-to-all | bytes 294912 | tf_op jit(solution)/shard_map/all_to_all | solution.py:17
  29.5 0.1 copy.10
  29.6 1.0 reshape.44
  30.6 0.0 all-gather.2.cloned.1.call-update
  30.6 0.0 reduce-scatter.2.cloned.1.call-start
  30.7 43.2 %all-gather.2.cloned.1.call-done = bf16[2,256,2304]{2,1,0:T(8,128)(2,1)} async-done(((bf16[2,16,2304]{2,1,0:T(8,128)(2,1)}), bf16[2,256,2304]{2,1,0:T(8,128)(2,1)}) %all-gather.2.cloned.1.call-update) | async-done | bytes 2359312 | tf_op jit(solution)/shard_map/all_gather | solution.py:19
  73.9 2.0 fusion.6
  75.9 0.0 copy-done.1
  75.9 0.6 fusion.7
  76.5 0.6 fusion.5
  77.2 0.2 fusion.24
  77.4 2.7 %fusion.3 = f32[2,256,2304]{2,1,0:T(8,128)S(1)} fusion(bf16[2304,256]{1,0:T(8,128)(2,1)S(1)} %copy-done.4, f32[1,256,256]{1,2,0:T(8,128)S(1)} %get-tuple-element.17, f32[1,256,256]{1,2,0:T(8,128)S(1)} %get-tuple-element.18), kind=kOutput, calls=%fused_computation.9 | convolution fusion | flops 1812070400 | bytes 6422528 | tf_op jit(solution)/shard_map/dot_general | solution.py:38
  80.1 4.0 %fusion.1 = f32[3,256,2304]{2,1,0:T(8,128)S(1)} fusion(bf16[2304,256]{1,0:T(8,128)(2,1)S(1)} %copy-done, f32[1,256,256]{1,2,0:T(8,128)S(1)} %get-tuple-element.14, f32[1,256,256]{1,2,0:T(8,128)S(1)} %get-tuple-element.18, f32[1,256,256]{1,2,0:T(8,128)S(1)} %get-tuple-element.13), kind=kOutput, calls=%fused_computation.7 | convolution fusion | flops 2718302208 | bytes 9043968 | tf_op jit(solution)/shard_map/dot_general | solution.py:45
  84.1 2.1 %slice_add_fusion.1 = (f32[1,256,2304]{2,1,0:T(8,128)S(1)}, f32[1,256,2304]{2,1,0:T(8,128)S(1)}, f32[1,256,2304]{2,1,0:T(8,128)}) fusion(f32[3,256,2304]{2,1,0:T(8,128)S(1)} %fusion.1, f32[2,256,2304]{2,1,0:T(8,128)S(1)} %fusion.3), kind=kLoop, calls=%fused_computation.3 | loop fusion | flops 1179648 | bytes 18874368 | tf_op jit(solution)/shard_map/add | solution.py:52
  86.2 5.1 %pad_maximum_fusion = f32[3,256,2304]{2,1,0:T(8,128)} fusion(f32[1,256,2304]{2,1,0:T(8,128)S(1)} %get-tuple-element.11, f32[1,256,2304]{2,1,0:T(8,128)} %get-tuple-element.12, f32[1,256,2304]{2,1,0:T(8,128)S(1)} %get-tuple-element.10), kind=kLoop, calls=%fused_computation | loop fusion | flops 3538944 | bytes 14155776 | tf_op jit(solution)/shard_map/stack | solution.py:52
  91.3 0.0 reduce-scatter.2.cloned.1.call-update
  91.4 25.1 %psum.21 = f32[2,256]{1,0:T(2,128)S(1)} all-reduce(f32[2,256]{1,0:T(2,128)S(1)} %pad_maximum_fusion.2), channel_id=1, replica_groups=mesh['tok'=16,'vy'=8,'vx'=4] {'tok'}, use_global_device_ids=true, to_apply=%region_2.0 | all-reduce | flops 512 | bytes 4096 | tf_op jit(solution)/shard_map/psum | solution.py:56
  116.5 16.9 %psum.22 = f32[2,256]{1,0:T(2,128)S(1)} all-reduce(f32[2,256]{1,0:T(2,128)S(1)} %psum.21), channel_id=1, replica_groups=mesh['tok'=16,'vy'=8,'vx'=4] {'vy'}, use_global_device_ids=true, to_apply=%region_3.0 | all-reduce | flops 512 | bytes 4096 | tf_op jit(solution)/shard_map/psum | solution.py:56
  133.4 8.8 %psum.23 = f32[2,256]{1,0:T(2,128)S(1)} all-reduce(f32[2,256]{1,0:T(2,128)S(1)} %psum.22), channel_id=1, replica_groups=mesh['tok'=16,'vy'=8,'vx'=4] {'vx'}, use_global_device_ids=true, to_apply=%region_4.0 | all-reduce | flops 512 | bytes 4096 | tf_op jit(solution)/shard_map/psum | solution.py:56
  142.2 19.3 %reduce-scatter.2.cloned.1.call-done = f32[3,16,2304]{2,1,0:T(8,128)} async-done(((f32[3,256,2304]{2,1,0:T(8,128)}), f32[3,16,2304]{2,1,0:T(8,128)}) %reduce-scatter.2.cloned.1.call-update) | async-done | bytes 442384 | tf_op jit(solution)/shard_map/reduce_scatter | solution.py:55
  161.5 2.7 %reshape.45 = f32[3,16,32,72]{3,2,1,0:T(8,128)} reshape(f32[3,16,2304]{2,1,0:T(8,128)} %reduce-scatter.2.cloned.1.call-done) | data formatting | bytes 884736 | tf_op jit(solution)/shard_map/reshape | solution.py:58
  164.2 2.5 %copy.19 = f32[3,16,32,72]{3,1,0,2:T(8,128)} copy(f32[3,16,32,72]{3,2,1,0:T(8,128)} %reshape.45) | data formatting | bytes 884736 | tf_op jit(solution)/shard_map/reshape | solution.py:58
  166.7 9.8 %all-to-all-start.1 = ((f32[32,3,16,72]{3,2,1,0:T(8,128)}), f32[32,3,16,72]{3,2,1,0:T(8,128)}, u32[]{:S(2)}, u32[]{:S(2)}) async-start(f32[32,3,16,72]{3,2,1,0:T(8,128)} %bitcast.66), calls=%async_computation.2 | async-start | bytes 1572864 | tf_op jit(solution)/shard_map/all_to_all | solution.py:59
  176.5 0.6 bitcast_divide_fusion.1
  177.1 1.2 fusion.26
  178.4 2.2 %convolution_bitcast_fusion = f32[2304,256]{1,0:T(8,128)} fusion(bf16[2,256,2304]{2,1,0:T(8,128)(2,1)S(1)} %copy-done.2, bf16[1,256,256]{1,2,0:T(8,128)(2,1)S(1)} %get-tuple-element.16, bf16[1,256,256]{1,2,0:T(8,128)(2,1)S(1)} %get-tuple-element.15), kind=kOutput, calls=%fused_computation.1 | convolution fusion | flops 604110848 | bytes 4980736 | tf_op jit(solution)/shard_map/krd,krv->dv/dot_general | solution.py:71
  180.6 15.3 %all-to-all-done.1 = f32[32,3,16,72]{3,2,1,0:T(8,128)} async-done(((f32[32,3,16,72]{3,2,1,0:T(8,128)}), f32[32,3,16,72]{3,2,1,0:T(8,128)}, u32[]{:S(2)}, u32[]{:S(2)}) %all-to-all-start.1) | async-done | bytes 442400 | tf_op jit(solution)/shard_map/all_to_all | solution.py:59
  196.0 1.2 reduce_sum.29
  197.2 0.7 fusion.27
  (19 shorter events, 0.1 us)
Async XLA Ops:
  7.2 66.7 %copy-start = (bf16[2304,256]{1,0:T(8,128)(2,1)S(1)}, bf16[2304,256]{1,0:T(8,128)(2,1)}, u32[]{:S(2)}) copy-start(bf16[2304,256]{1,0:T(8,128)(2,1)} %param.6) | copy-start | bytes 3538948
  7.2 66.7 %all-gather.2.cloned.1.call-start = ((), (), s32[]{:S(2)}) async-start(), calls=%async_computation.3 | async-start | bytes 2506752 | tf_op jit(solution)/shard_map/all_gather | solution.py:19
  8.0 67.9 %copy-start.4 = (bf16[2304,256]{1,0:T(8,128)(2,1)S(1)}, bf16[2304,256]{1,0:T(8,128)(2,1)}, u32[]{:S(2)}) copy-start(bf16[2304,256]{1,0:T(8,128)(2,1)} %param.9) | copy-start | bytes 3538948
  30.6 130.9 %reduce-scatter.2.cloned.1.call-start = ((), (), s32[]{:S(2)}) async-start(), calls=%async_computation.4 | async-start | bytes 7520256 | tf_op jit(solution)/shard_map/reduce_scatter | solution.py:55
  73.9 2.0 copy-start.1
  75.9 1.2 copy-start.5
  75.9 1.2 copy-start.6
  77.2 3.0 %copy-start.3 = (f32[256,256]{0,1:T(8,128)}, f32[256,256]{0,1:T(8,128)S(1)}, u32[]{:S(2)}) copy-start(f32[256,256]{0,1:T(8,128)S(1)} %fusion.5) | copy-start | bytes 786436
  142.2 36.2 %copy-start.2 = (bf16[2,256,2304]{2,1,0:T(8,128)(2,1)S(1)}, bf16[2,256,2304]{2,1,0:T(8,128)(2,1)}, u32[]{:S(2)}) copy-start(bf16[2,256,2304]{2,1,0:T(8,128)(2,1)} %all-gather.2.cloned.1.call-done) | copy-start | bytes 7077892
  166.7 29.3 %all-to-all-start.1 = ((f32[32,3,16,72]{3,2,1,0:T(8,128)}), f32[32,3,16,72]{3,2,1,0:T(8,128)}, u32[]{:S(2)}, u32[]{:S(2)}) async-start(f32[32,3,16,72]{3,2,1,0:T(8,128)} %bitcast.66), calls=%async_computation.2 | async-start | bytes 1572864 | tf_op jit(solution)/shard_map/all_to_all | solution.py:59
  178.4 18.8 %copy-start.7 = (f32[16]{0:T(128)S(1)}, f32[16]{0:T(128)}, u32[]{:S(2)}) copy-start(f32[16]{0:T(128)} %get-tuple-element.20) | copy-start | bytes 196
Sparse Core Ops, SparseCore 0:
  30.7 43.1 all-gather.1
  91.5 69.9 reduce-scatter.1
where the time goes:
time: 205 us
  waiting for transfers between devices  77.8 us (38%)
  blocking collectives  72.2 us (35%)
  between operations  14.2 us (7%)
  matrix products  12.1 us (6%)
  other arithmetic  12 us (6%)
  starting transfers between devices  9.91 us (5%)
  local copies, waits for them, and re-layouts  6.41 us (3%)
    psum x3, blocking collectives, local(): stats = lax.psum(lax.psum(lax.psum(local_stats, 'tok'), 'vy'), 'vx')  50.8 us
    all_gather x1, waiting for transfers between devices, local(): gathered = lax.all_gather(features, 'tok', axis=1, tiled=True)  43.2 us
    all_to_all x1, blocking collectives, local(): blocks = lax.all_to_all(copies, ('vy', 'vx'), 0, 0, tiled=True)  21.4 us
    reduce_scatter x1, waiting for transfers between devices, local(): summed = lax.psum_scatter(partials, 'tok', scatter_dimension=1, tiled=True)  19.3 us
    all_to_all x1, waiting for transfers between devices, local(): lax.all_to_all(blocks, ('vy', 'vx'), 0, 0, tiled=True)  15.3 us
    all_to_all x1, starting transfers between devices, local(): lax.all_to_all(blocks, ('vy', 'vx'), 0, 0, tiled=True)  9.83 us
    reshape x2, local copies, waits for them, and re-layouts, local(): summed.reshape(kinds, rows, voc_count, width // voc_count)  5.19 us
    another operation x1, other arithmetic, local(): jnp.stack([by_probe[0] + by_head[0], by_head[1], by_probe[1] + by_head[2]])  5.14 us
  transfers between devices with their start and end apart: 3, of which 3 were waited for; matrix products, arithmetic and copies ran while one was open for 2% of the time, Pallas kernels for 0%

commit v1 on v0

--- a/solution.py
+++ b/solution.py
@@ -16,7 +16,9 @@
     copies = jnp.broadcast_to(stacked[None], (voc_count,) + stacked.shape)
     blocks = lax.all_to_all(copies, ("vy", "vx"), 0, 0, tiled=True)
     features = blocks.transpose(1, 2, 0, 3).reshape(2, rows_here, voc_count * stacked.shape[2])
-    gathered = lax.all_gather(features, "tok", axis=1, tiled=True)
+    gathered = jnp.concatenate(
+        lax.all_to_all(jnp.stack([features] * lax.axis_size("tok")), "tok", 0, 0), axis=1
+    )
     row_hidden = gathered[0]
     row_probe = gathered[1]
     logits = jnp.dot(row_hidden, head, preferred_element_type=jnp.float32)

time: 205 us -> 227 us (1.11)
  starting transfers between devices: 9.91 us -> 20.4 us
  waiting for transfers between devices: 77.8 us -> 88 us
  local copies, waits for them, and re-layouts: 6.41 us -> 9.88 us
    all_to_all x0 -> x1, waiting for transfers between devices: none -> 54.9 us  [local(): lax.all_to_all(jnp.stack([features] * lax.axis_size('tok')), 'tok', 0, 0)]
    all_gather x1 -> x0, waiting for transfers between devices: 43.2 us -> none  [local(): gathered = lax.all_gather(features, 'tok', axis=1, tiled=True)]
    all_to_all x0 -> x1, starting transfers between devices: none -> 10.5 us  [local(): lax.all_to_all(jnp.stack([features] * lax.axis_size('tok')), 'tok', 0, 0)]
where the time goes in v1:
time: 227 us
  waiting for transfers between devices  88 us (39%)
  blocking collectives  70.4 us (31%)
  starting transfers between devices  20.4 us (9%)
  between operations  14.2 us (6%)
  other arithmetic  12.9 us (6%)
  matrix products  10.7 us (5%)
  local copies, waits for them, and re-layouts  9.88 us (4%)
    all_to_all x1, waiting for transfers between devices, local(): lax.all_to_all(jnp.stack([features] * lax.axis_size('tok')), 'tok', 0, 0)  54.9 us
    psum x3, blocking collectives, local(): stats = lax.psum(lax.psum(lax.psum(local_stats, 'tok'), 'vy'), 'vx')  49.1 us
    all_to_all x1, blocking collectives, local(): blocks = lax.all_to_all(copies, ('vy', 'vx'), 0, 0, tiled=True)  21.3 us
    reduce_scatter x1, waiting for transfers between devices, local(): summed = lax.psum_scatter(partials, 'tok', scatter_dimension=1, tiled=True)  17.1 us
    all_to_all x1, waiting for transfers between devices, local(): lax.all_to_all(blocks, ('vy', 'vx'), 0, 0, tiled=True)  15.9 us
    all_to_all x1, starting transfers between devices, local(): lax.all_to_all(jnp.stack([features] * lax.axis_size('tok')), 'tok', 0, 0)  10.5 us
    all_to_all x1, starting transfers between devices, local(): lax.all_to_all(blocks, ('vy', 'vx'), 0, 0, tiled=True)  9.93 us
    another operation x1, other arithmetic, local(): jnp.stack([by_probe[0] + by_head[0], by_head[1], by_probe[1] + by_head[2]])  5.74 us
  transfers between devices with their start and end apart: 3, of which 3 were waited for; matrix products, arithmetic and copies ran while one was open for 2% of the time, Pallas kernels for 0%

profile of v1, /device:TPU:2, one launch (start us, length us, event | category | flops | bytes accessed | tf_op | source)
XLA Modules:
  0.0 226.6 jit_solution(7275496071067780263)
XLA Ops:
  7.2 0.8 pad_maximum_fusion.1
  8.0 21.3 %all_to_all.15 = bf16[32,2,16,72]{3,2,1,0:T(8,128)(2,1)S(1)} all-to-all(bf16[32,2,16,72]{3,2,1,0:T(8,128)(2,1)S(1)} %broadcast_in_dim.2), channel_id=1, replica_groups=mesh['tok'=16,'vy'=8,'vx'=4] {'vy','vx'}, dimensions={0} | all-to-all | bytes 294912 | tf_op jit(solution)/shard_map/all_to_all | solution.py:17
  29.3 0.1 copy.21
  29.4 0.4 stack_reshape.2
  29.7 1.6 stack.57
  31.4 10.5 %all-to-all-start.1 = ((bf16[16,2,16,2304]{3,2,1,0:T(8,128)(2,1)}), bf16[16,2,16,2304]{3,2,1,0:T(8,128)(2,1)}, u32[]{:S(2)}, u32[]{:S(2)}) async-start(bf16[16,2,16,2304]{3,2,1,0:T(8,128)(2,1)} %stack.57), calls=%async_computation.1 | async-start | bytes 4718592 | tf_op jit(solution)/shard_map/all_to_all | solution.py:20
  41.9 0.0 reduce-scatter.2.cloned.1.call-start
  41.9 54.9 %all-to-all-done.1 = bf16[16,2,16,2304]{3,2,1,0:T(8,128)(2,1)} async-done(((bf16[16,2,16,2304]{3,2,1,0:T(8,128)(2,1)}), bf16[16,2,16,2304]{3,2,1,0:T(8,128)(2,1)}, u32[]{:S(2)}, u32[]{:S(2)}) %all-to-all-start.1) | async-done | bytes 2359328 | tf_op jit(solution)/shard_map/all_to_all | solution.py:20
  96.9 1.8 copy.36
  98.7 0.2 fusion.31
  98.9 0.6 fusion.33
  99.5 0.6 fusion.4
  100.2 0.6 convolution_add_fusion
  100.8 0.2 fusion.21
  101.0 0.5 copy-done.3
  101.5 2.7 %fusion.2 = f32[2,256,2304]{2,1,0:T(8,128)S(1)} fusion(bf16[2304,256]{1,0:T(8,128)(2,1)S(1)} %copy-done.1, f32[1,256,256]{1,2,0:T(8,128)S(1)} %get-tuple-element.21, f32[1,256,256]{1,2,0:T(8,128)S(1)} %get-tuple-element.22), kind=kOutput, calls=%fused_computation.6 | convolution fusion | flops 1812070400 | bytes 6422528 | tf_op jit(solution)/shard_map/dot_general | solution.py:40
  104.2 4.0 %fusion = f32[3,256,2304]{2,1,0:T(8,128)S(1)} fusion(bf16[2304,256]{1,0:T(8,128)(2,1)S(1)} %copy-done, f32[1,256,256]{1,2,0:T(8,128)S(1)} %get-tuple-element.18, f32[1,256,256]{1,2,0:T(8,128)S(1)} %get-tuple-element.22, f32[1,256,256]{1,2,0:T(8,128)S(1)} %get-tuple-element.17), kind=kOutput, calls=%fused_computation.4 | convolution fusion | flops 2718302208 | bytes 9043968 | tf_op jit(solution)/shard_map/dot_general | solution.py:47
  108.2 3.0 %slice_add_fusion.1 = (f32[1,256,2304]{2,1,0:T(8,128)S(1)}, f32[1,256,2304]{2,1,0:T(8,128)}, f32[1,256,2304]{2,1,0:T(8,128)}) fusion(f32[3,256,2304]{2,1,0:T(8,128)S(1)} %fusion, f32[2,256,2304]{2,1,0:T(8,128)S(1)} %fusion.2), kind=kLoop, calls=%fused_computation.3 | loop fusion | flops 1179648 | bytes 18874368 | tf_op jit(solution)/shard_map/add | solution.py:54
  111.2 5.7 %pad_maximum_fusion = f32[3,256,2304]{2,1,0:T(8,128)} fusion(f32[1,256,2304]{2,1,0:T(8,128)} %get-tuple-element.11, f32[1,256,2304]{2,1,0:T(8,128)} %get-tuple-element.12, f32[1,256,2304]{2,1,0:T(8,128)S(1)} %get-tuple-element.10), kind=kLoop, calls=%fused_computation | loop fusion | flops 3538944 | bytes 14155776 | tf_op jit(solution)/shard_map/stack | solution.py:54
  116.9 24.1 %psum.21 = f32[2,256]{1,0:T(2,128)S(1)} all-reduce(f32[2,256]{1,0:T(2,128)S(1)} %pad_maximum_fusion.2), channel_id=1, replica_groups=mesh['tok'=16,'vy'=8,'vx'=4] {'tok'}, use_global_device_ids=true, to_apply=%region_2.0 | all-reduce | flops 512 | bytes 4096 | tf_op jit(solution)/shard_map/psum | solution.py:58
  141.0 15.5 %psum.22 = f32[2,256]{1,0:T(2,128)S(1)} all-reduce(f32[2,256]{1,0:T(2,128)S(1)} %psum.21), channel_id=1, replica_groups=mesh['tok'=16,'vy'=8,'vx'=4] {'vy'}, use_global_device_ids=true, to_apply=%region_3.0 | all-reduce | flops 512 | bytes 4096 | tf_op jit(solution)/shard_map/psum | solution.py:58
  156.5 9.5 %psum.23 = f32[2,256]{1,0:T(2,128)S(1)} all-reduce(f32[2,256]{1,0:T(2,128)S(1)} %psum.22), channel_id=1, replica_groups=mesh['tok'=16,'vy'=8,'vx'=4] {'vx'}, use_global_device_ids=true, to_apply=%region_4.0 | all-reduce | flops 512 | bytes 4096 | tf_op jit(solution)/shard_map/psum | solution.py:58
  166.1 17.1 %reduce-scatter.2.cloned.1.call-done = f32[3,16,2304]{2,1,0:T(8,128)} async-done(((f32[3,256,2304]{2,1,0:T(8,128)}), f32[3,16,2304]{2,1,0:T(8,128)}) %reduce-scatter.2.cloned.1.call-update) | async-done | bytes 442384 | tf_op jit(solution)/shard_map/reduce_scatter | solution.py:57
  183.2 2.7 %reshape.55 = f32[3,16,32,72]{3,2,1,0:T(8,128)} reshape(f32[3,16,2304]{2,1,0:T(8,128)} %reduce-scatter.2.cloned.1.call-done) | data formatting | bytes 884736 | tf_op jit(solution)/shard_map/reshape | solution.py:60
  185.9 2.5 %copy.35 = f32[3,16,32,72]{3,1,0,2:T(8,128)} copy(f32[3,16,32,72]{3,2,1,0:T(8,128)} %reshape.55) | data formatting | bytes 884736 | tf_op jit(solution)/shard_map/reshape | solution.py:60
  188.4 9.9 %all-to-all-start.2 = ((f32[32,3,16,72]{3,2,1,0:T(8,128)}), f32[32,3,16,72]{3,2,1,0:T(8,128)}, u32[]{:S(2)}, u32[]{:S(2)}) async-start(f32[32,3,16,72]{3,2,1,0:T(8,128)} %bitcast.72), calls=%async_computation.3 | async-start | bytes 1572864 | tf_op jit(solution)/shard_map/all_to_all | solution.py:61
  198.3 0.1 bitcast_divide_fusion.1
  198.4 1.2 fusion.23
  199.7 2.2 convolution_bitcast_fusion
  201.9 15.9 %all-to-all-done.2 = f32[32,3,16,72]{3,2,1,0:T(8,128)} async-done(((f32[32,3,16,72]{3,2,1,0:T(8,128)}), f32[32,3,16,72]{3,2,1,0:T(8,128)}, u32[]{:S(2)}, u32[]{:S(2)}) %all-to-all-start.2) | async-done | bytes 442400 | tf_op jit(solution)/shard_map/all_to_all | solution.py:61
  217.9 1.2 reduce_sum.29
  219.1 0.7 fusion.24
  (17 shorter events, 0.2 us)
Async XLA Ops:
  7.2 91.7 %copy-start = (bf16[2304,256]{1,0:T(8,128)(2,1)S(1)}, bf16[2304,256]{1,0:T(8,128)(2,1)}, u32[]{:S(2)}) copy-start(bf16[2304,256]{1,0:T(8,128)(2,1)} %param.6) | copy-start | bytes 3538948
  31.4 65.5 %all-to-all-start.1 = ((bf16[16,2,16,2304]{3,2,1,0:T(8,128)(2,1)}), bf16[16,2,16,2304]{3,2,1,0:T(8,128)(2,1)}, u32[]{:S(2)}, u32[]{:S(2)}) async-start(bf16[16,2,16,2304]{3,2,1,0:T(8,128)(2,1)} %stack.57), calls=%async_computation.1 | async-start | bytes 4718592 | tf_op jit(solution)/shard_map/all_to_all | solution.py:20
  41.9 141.3 %reduce-scatter.2.cloned.1.call-start = ((), (), s32[]{:S(2)}) async-start(), calls=%async_computation.4 | async-start | bytes 7520256 | tf_op jit(solution)/shard_map/reduce_scatter | solution.py:57
  41.9 58.8 %copy-start.5 = (s32[256]{0:T(256)}, s32[256]{0:T(256)S(1)}, u32[]{:S(2)}) copy-start(s32[256]{0:T(256)S(1)} %iota_add_fusion) | copy-start | bytes 3076
  98.9 1.3 copy-start.1
  99.5 1.3 copy-start.4
  100.2 0.8 copy-start.2
  100.8 0.7 copy-start.3
  188.4 29.5 %all-to-all-start.2 = ((f32[32,3,16,72]{3,2,1,0:T(8,128)}), f32[32,3,16,72]{3,2,1,0:T(8,128)}, u32[]{:S(2)}, u32[]{:S(2)}) async-start(f32[32,3,16,72]{3,2,1,0:T(8,128)} %bitcast.72), calls=%async_computation.3 | async-start | bytes 1572864 | tf_op jit(solution)/shard_map/all_to_all | solution.py:61
Sparse Core Ops, SparseCore 0:
  117.0 66.0 reduce-scatter.1
